TPU v7x, 128 devices: a whole 4x4x4 slice. The times are simulated.
128 devices in a mesh: ctx: 16 (over y_hi, x, core), head: 8 (over y_lo, z).
Axes of the slice: x: 4, y: 4 (y_hi: 2, y_lo: 2; y = y_hi * 2 + y_lo), z: 4, core: 2. Of those that a mesh axis runs over, the one named last changes fastest.
Arguments:
- block_order: int32 [32], replicated, may hold values from 0 to 31, each once
- queries: bfloat16 [3584, 64, 576], P('ctx', 'head'), may hold values from -10 to 10
- keys: bfloat16 [3584, 576], P('ctx'), may hold values from -4 to 4
- dout: bfloat16 [3584, 64, 512], P('ctx', 'head'), may hold values from -6 to 6
Outputs:
- grad_queries: bfloat16 [3584, 64, 576], P('ctx', 'head')
- grad_keys: float32 [3584, 576], P('ctx')
Inputs may be any that keep to these rules, and one draw needn't show every extreme that they name: block_order holds each of 0 to 31 once.
All inputs are finite; a program needn't handle non-finite values.
Results may differ from a plain program's by a relative error of at most 0.0048.
Values may be sent and summed in bfloat16 or wider, within the bound.
A program may use at most 64 MiB of HBM per device.

v0:
```python
import jax
import jax.numpy as jnp
from jax import lax
from jax.sharding import PartitionSpec as P

softmax_scale = 0.1352
masked_value = -1e30


def per_device(block_order, queries, keys, dout):
    token_count, head_count, key_width = queries.shape
    latent_width = dout.shape[2]
    block_rows = token_count // 2
    ctx_index = lax.axis_index("ctx")
    offsets = jnp.arange(block_rows, dtype=jnp.int32)
    all_positions = (block_order[:, None] * block_rows + offsets[None, :]).reshape(-1)
    own_positions = lax.dynamic_slice_in_dim(all_positions, ctx_index * token_count, token_count)
    row_positions = jnp.repeat(own_positions, head_count)
    query_last = jnp.max(own_positions)
    query_rows = queries.reshape(token_count * head_count, key_width)
    grad_rows = dout.reshape(token_count * head_count, latent_width)
    row_count = query_rows.shape[0]
    seq_length = token_count * lax.axis_size("ctx")
    contract_rows = (((0,), (0,)), ((), ()))

    def block_scores(key_block, key_pos):
        scores = (
            jnp.dot(query_rows, key_block.T, preferred_element_type=jnp.float32) * softmax_scale
        )
        return jnp.where(key_pos[None, :] <= row_positions[:, None], scores, masked_value)

    def split_piece(piece):
        count = piece.shape[0] // token_count
        return (
            piece.reshape(count, token_count, key_width),
            all_positions.reshape(count, token_count),
        )

    def make_second(peak, total, delta):

        def second_fold(carry, piece, start):
            grad_query, grad_keys = carry
            blocks, positions = split_piece(piece)

            def second_visit(accum, items):
                key_block, key_pos = items

                def second_compute(accum):
                    scores = block_scores(key_block, key_pos)
                    probs = jnp.exp(scores - peak[:, None]) / total[:, None]
                    grad_probs = jnp.dot(
                        grad_rows, key_block[:, :latent_width].T, preferred_element_type=jnp.float32
                    )
                    grad_scores = (probs * (grad_probs - delta[:, None])).astype(jnp.bfloat16)
                    probs_half = probs.astype(jnp.bfloat16)
                    accum = (
                        accum
                        + jnp.dot(grad_scores, key_block, preferred_element_type=jnp.float32)
                        * softmax_scale
                    )
                    key_part = (
                        lax.dot_general(
                            grad_scores,
                            query_rows,
                            contract_rows,
                            preferred_element_type=jnp.float32,
                        )
                        * softmax_scale
                    )
                    value_part = lax.dot_general(
                        probs_half, grad_rows, contract_rows, preferred_element_type=jnp.float32
                    )
                    return (
                        accum,
                        key_part + jnp.pad(value_part, ((0, 0), (0, key_width - latent_width))),
                    )

                def skip(accum):
                    return (accum, jnp.zeros((token_count, key_width), jnp.float32))

                return lax.cond(jnp.min(key_pos) <= query_last, second_compute, skip, accum)

            grad_query, key_terms = lax.scan(second_visit, grad_query, (blocks, positions))
            length = piece.shape[0]
            grad_keys = key_terms.reshape(length, key_width)
            return (grad_query, grad_keys)

        return second_fold

    start_state = (
        jnp.full((row_count,), masked_value, jnp.float32),
        jnp.zeros((row_count,), jnp.float32),
        jnp.zeros((row_count,), jnp.float32),
    )
    second_start = (
        jnp.zeros((row_count, key_width), jnp.float32),
        jnp.zeros((seq_length, key_width), jnp.float32),
    )
    carry = start_state
    blocks, positions = split_piece(lax.all_gather(keys, "ctx", axis=0, tiled=True))

    def first_visit(state, items):
        key_block, key_pos = items

        def first_compute(state):
            peak, total, weighted = state
            scores = block_scores(key_block, key_pos)
            grad_probs = jnp.dot(
                grad_rows, key_block[:, :latent_width].T, preferred_element_type=jnp.float32
            )
            new_peak = jnp.maximum(peak, jnp.max(scores, axis=1))
            factor = jnp.exp(peak - new_peak)
            weights = jnp.exp(scores - new_peak[:, None])
            total = total * factor + jnp.sum(weights, axis=1)
            weighted = weighted * factor + jnp.sum(weights * grad_probs, axis=1)
            return (new_peak, total, weighted)

        def keep(state):
            return state

        return (lax.cond(jnp.min(key_pos) <= query_last, first_compute, keep, state), None)

    carry, unused = lax.scan(first_visit, carry, (blocks, positions))
    peak, total, weighted = carry
    second_fold = make_second(peak, total, weighted / total)
    grad_query, grad_keys = second_fold(
        second_start, lax.all_gather(keys, "ctx", axis=0, tiled=True), jnp.int32(0)
    )
    grad_queries = grad_query.reshape(token_count, head_count, key_width).astype(jnp.bfloat16)
    own_terms = lax.psum_scatter(grad_keys, "ctx", scatter_dimension=0, tiled=True)
    key_result = lax.psum(own_terms, "head")
    return (grad_queries, key_result)


def solution(mesh):
    placed = (P(), P("ctx", "head", None), P("ctx", None), P("ctx", "head", None))
    return jax.shard_map(
        per_device,
        mesh=mesh,
        in_specs=placed,
        out_specs=(P("ctx", "head", None), P("ctx", None)),
        check_vma=False,
    )
```

profile of v0, /device:TPU:0, one launch (start us, length us, event | category | flops | bytes accessed | tf_op | source)
XLA Modules:
  0.0 600.2 jit_solution(2105240949158212985)
XLA Ops:
  9.9 60.6 %all-gather.2.cloned.1.call-done = bf16[3584,576]{1,0:T(8,128)(2,1)} async-done(((bf16[224,576]{1,0:T(8,128)(2,1)}), bf16[3584,576]{1,0:T(8,128)(2,1)}) %all-gather.2.cloned.1.call-update) | async-done | bytes 4128784 | tf_op jit(solution)/shard_map/all_gather | solution.py:127
  70.5 69.5 %while.31 = (s32[]{:T(128)}, f32[1792]{0:T(1024)S(1)}, f32[1792]{0:T(1024)S(1)}, f32[1792]{0:T(1024)S(1)}, s32[16,224]{1,0:T(8,128)S(1)}, /*index=5*/s32[]{:T(12...) while((s32[]{:T(128)}, f32[1792]{0:T(1024)S(1)}, ...), condition=%wide.region_8.9_spmd.clone, body=%wide.region_1.8_spmd.clone.sunk | while | flops 877082112 | bytes 17222444 | solution.py:123
  72.4 5.0 conditional.6
  82.9 5.0 conditional.6
  91.6 5.0 conditional.6
  92.8 2.7 fusion.26
  98.4 5.0 conditional.6
  99.7 2.7 fusion.26
  110.9 5.0 conditional.6
  119.6 5.0 conditional.6
  126.4 5.0 conditional.6
  133.2 5.0 conditional.6
  134.4 2.7 fusion.26
  142.3 136.9 %while.32 = (s32[]{:T(128)}, f32[1792,576]{0,1:T(8,128)}, f32[16,224,576]{2,1,0:T(8,128)}, s32[16,224]{1,0:T(8,128)S(1)}, s32[]{:T(128)}, /*index=5*/bf16[16,224...) while((s32[]{:T(128)}, f32[1792,576]{0,1:T(8,128)}, ...), condition=%wide.region_13.14_spmd.clone, body=%wide.region_9.13_spmd.clone.sunk | while | flops 2215284992 | bytes 68409680 | solution.py:83
  144.2 11.5 %conditional.7 = (f32[1792,576]{0,1:T(8,128)}, f32[1,224,576]{2,1,0:T(8,128)S(1)}) conditional(s32[]{:T(128)} %convert_element_type.32, f32[1792,576]{0,1:T(8,128)} %get-tuple-element.560, (s32[1,224]{1,0:T(1,128)S(1)}, s32[224]{0:T(256)S(1)}, bf16[16,224,576]{2,1,0:T(8,128)(2,1)}, s32[]{:T(128)}, bf16[1792,576]{1,0:T(8,128)(2,1)}, ...), branch_computations={%region_11.11_spmd, %region_12.12_spmd} | conditional | flops 2215284736 | bytes 67317608 | solution.py:81
  164.2 11.5 %conditional.7 = (f32[1792,576]{0,1:T(8,128)}, f32[1,224,576]{2,1,0:T(8,128)S(1)}) conditional(s32[]{:T(128)} %convert_element_type.32, f32[1792,576]{0,1:T(8,128)} %get-tuple-element.560, (s32[1,224]{1,0:T(1,128)S(1)}, s32[224]{0:T(256)S(1)}, bf16[16,224,576]{2,1,0:T(8,128)(2,1)}, s32[]{:T(128)}, bf16[1792,576]{1,0:T(8,128)(2,1)}, ...), branch_computations={%region_11.11_spmd, %region_12.12_spmd} | conditional | flops 2215284736 | bytes 67317608 | solution.py:81
  181.3 11.5 %conditional.7 = (f32[1792,576]{0,1:T(8,128)}, f32[1,224,576]{2,1,0:T(8,128)S(1)}) conditional(s32[]{:T(128)} %convert_element_type.32, f32[1792,576]{0,1:T(8,128)} %get-tuple-element.560, (s32[1,224]{1,0:T(1,128)S(1)}, s32[224]{0:T(256)S(1)}, bf16[16,224,576]{2,1,0:T(8,128)(2,1)}, s32[]{:T(128)}, bf16[1792,576]{1,0:T(8,128)(2,1)}, ...), branch_computations={%region_11.11_spmd, %region_12.12_spmd} | conditional | flops 2215284736 | bytes 67317608 | solution.py:81
  195.5 11.5 %conditional.7 = (f32[1792,576]{0,1:T(8,128)}, f32[1,224,576]{2,1,0:T(8,128)S(1)}) conditional(s32[]{:T(128)} %convert_element_type.32, f32[1792,576]{0,1:T(8,128)} %get-tuple-element.560, (s32[1,224]{1,0:T(1,128)S(1)}, s32[224]{0:T(256)S(1)}, bf16[16,224,576]{2,1,0:T(8,128)(2,1)}, s32[]{:T(128)}, bf16[1792,576]{1,0:T(8,128)(2,1)}, ...), branch_computations={%region_11.11_spmd, %region_12.12_spmd} | conditional | flops 2215284736 | bytes 67317608 | solution.py:81
  218.3 11.5 %conditional.7 = (f32[1792,576]{0,1:T(8,128)}, f32[1,224,576]{2,1,0:T(8,128)S(1)}) conditional(s32[]{:T(128)} %convert_element_type.32, f32[1792,576]{0,1:T(8,128)} %get-tuple-element.560, (s32[1,224]{1,0:T(1,128)S(1)}, s32[224]{0:T(256)S(1)}, bf16[16,224,576]{2,1,0:T(8,128)(2,1)}, s32[]{:T(128)}, bf16[1792,576]{1,0:T(8,128)(2,1)}, ...), branch_computations={%region_11.11_spmd, %region_12.12_spmd} | conditional | flops 2215284736 | bytes 67317608 | solution.py:81
  235.4 11.5 %conditional.7 = (f32[1792,576]{0,1:T(8,128)}, f32[1,224,576]{2,1,0:T(8,128)S(1)}) conditional(s32[]{:T(128)} %convert_element_type.32, f32[1792,576]{0,1:T(8,128)} %get-tuple-element.560, (s32[1,224]{1,0:T(1,128)S(1)}, s32[224]{0:T(256)S(1)}, bf16[16,224,576]{2,1,0:T(8,128)(2,1)}, s32[]{:T(128)}, bf16[1792,576]{1,0:T(8,128)(2,1)}, ...), branch_computations={%region_11.11_spmd, %region_12.12_spmd} | conditional | flops 2215284736 | bytes 67317608 | solution.py:81
  249.7 11.5 %conditional.7 = (f32[1792,576]{0,1:T(8,128)}, f32[1,224,576]{2,1,0:T(8,128)S(1)}) conditional(s32[]{:T(128)} %convert_element_type.32, f32[1792,576]{0,1:T(8,128)} %get-tuple-element.560, (s32[1,224]{1,0:T(1,128)S(1)}, s32[224]{0:T(256)S(1)}, bf16[16,224,576]{2,1,0:T(8,128)(2,1)}, s32[]{:T(128)}, bf16[1792,576]{1,0:T(8,128)(2,1)}, ...), branch_computations={%region_11.11_spmd, %region_12.12_spmd} | conditional | flops 2215284736 | bytes 67317608 | solution.py:81
  263.9 11.5 %conditional.7 = (f32[1792,576]{0,1:T(8,128)}, f32[1,224,576]{2,1,0:T(8,128)S(1)}) conditional(s32[]{:T(128)} %convert_element_type.32, f32[1792,576]{0,1:T(8,128)} %get-tuple-element.560, (s32[1,224]{1,0:T(1,128)S(1)}, s32[224]{0:T(256)S(1)}, bf16[16,224,576]{2,1,0:T(8,128)(2,1)}, s32[]{:T(128)}, bf16[1792,576]{1,0:T(8,128)(2,1)}, ...), branch_computations={%region_11.11_spmd, %region_12.12_spmd} | conditional | flops 2215284736 | bytes 67317608 | solution.py:81
  279.3 235.7 %reduce-scatter.2.cloned.1.call-done = f32[224,576]{1,0:T(8,128)} async-done(((f32[3584,576]{1,0:T(8,128)}), f32[224,576]{1,0:T(8,128)}) %reduce-scatter.2.cloned.1.call-update) | async-done | bytes 516112 | tf_op jit(solution)/shard_map/reduce_scatter | solution.py:130
  520.0 71.8 %all-reduce.3.cloned.1.call-done = f32[224,576]{1,0:T(8,128)} async-done(((f32[224,576]{1,0:T(8,128)}), f32[224,576]{1,0:T(8,128)}) %all-reduce.3.cloned.1.call-update) | async-done | bytes 516112 | tf_op jit(solution)/shard_map/psum | solution.py:131
  (296 shorter events, 169.5 us)
Async XLA Ops:
  7.2 63.4 %all-gather.2.cloned.1.call-start = ((), (), s32[]{:S(2)}) async-start(), calls=%async_computation.1 | async-start | bytes 4874240 | tf_op jit(solution)/shard_map/all_gather | solution.py:127
  7.9 507.1 %reduce-scatter.2.cloned.1.call-start = ((), (), s32[]{:S(2)}) async-start(), calls=%async_computation.2 | async-start | bytes 9748480 | tf_op jit(solution)/shard_map/reduce_scatter | solution.py:130
  73.6 2.7 copy-start.2
  84.1 2.7 copy-start.2
  92.8 2.7 copy-start.2
  99.6 2.7 copy-start.2
  112.1 2.7 copy-start.2
  120.8 2.7 copy-start.2
  127.6 2.7 copy-start.2
  134.4 2.7 copy-start.2
  140.1 2.2 copy-start.3
  150.3 2.2 copy-start
  170.2 2.2 copy-start
  187.4 2.2 copy-start
  201.6 2.2 copy-start
  224.4 2.2 copy-start
  227.9 1.9 copy-start.1
  241.5 2.2 copy-start
  245.0 1.9 copy-start.1
  255.8 2.2 copy-start
  259.3 1.9 copy-start.1
  270.0 2.2 copy-start
  273.5 1.9 copy-start.1
  279.2 312.6 %all-reduce.3.cloned.1.call-start = ((), (), s32[]{:S(2)}) async-start(), calls=%async_computation.3 | async-start | bytes 1146880 | tf_op jit(solution)/shard_map/psum | solution.py:131
  (12 other events, 20.9 us)
Sparse Core Ops, SparseCore 0:
  10.4 60.0 all-gather.1
  279.4 235.6 reduce-scatter.1
  517.5 74.2 all-reduce.2
where the time goes:
time: 604 us; the launch traced here: 600 us
  waiting for transfers between devices  369 us (61%)
  matrix products  76.1 us (13%)
  local copies, waits for them, and re-layouts  73.3 us (12%)
  loops' own time  41.3 us (7%)
  other arithmetic  26.7 us (4%)
  between operations  13.8 us (2%)
    reduce_scatter x1, waiting for transfers between devices, per_device(): lax.psum_scatter(grad_keys, 'ctx', scatter_dimension=0, tiled=True)  236 us
    psum x1, waiting for transfers between devices, per_device(): key_result = lax.psum(own_terms, 'head')  71.8 us
    all_gather x1, waiting for transfers between devices, per_device(): lax.all_gather(keys, 'ctx', axis=0, tiled=True)  60.6 us
    dot_general x16, matrix products, block_scores(): jnp.dot(query_rows, key_block.T, preferred_element_type=jnp.float32)  42 us
    cond x72, local copies, waits for them, and re-layouts  33.3 us
    another operation x1, loops' own time, second_fold(): lax.scan(second_visit, grad_query, (blocks, positions))  20.3 us
    another operation x1, loops' own time, per_device(): carry, unused = lax.scan(first_visit, carry, (blocks, positions))  19.4 us
    squeeze x16, local copies, waits for them, and re-layouts, per_device(): carry, unused = lax.scan(first_visit, carry, (blocks, positions))  15.8 us
  transfers between devices with their start and end apart: 3, of which 3 were waited for; matrix products, arithmetic and copies ran while one was open for 1% of the time, Pallas kernels for 0%

commit v1 on v0

--- a/solution.py
+++ b/solution.py
@@ -124,7 +124,11 @@
     peak, total, weighted = carry
     second_fold = make_second(peak, total, weighted / total)
     grad_query, grad_keys = second_fold(
-        second_start, lax.all_gather(keys, "ctx", axis=0, tiled=True), jnp.int32(0)
+        second_start,
+        jnp.concatenate(
+            lax.all_to_all(jnp.stack([keys] * lax.axis_size("ctx")), "ctx", 0, 0), axis=0
+        ),
+        jnp.int32(0),
     )
     grad_queries = grad_query.reshape(token_count, head_count, key_width).astype(jnp.bfloat16)
     own_terms = lax.psum_scatter(grad_keys, "ctx", scatter_dimension=0, tiled=True)

time: 604 us -> 634 us (1.050)
  waiting for transfers between devices: 369 us -> 385 us
  starting transfers between devices: 0.12 us -> 7.42 us
    all_gather x1, waiting for transfers between devices: 60.6 us -> 81.6 us  [per_device(): lax.all_gather(keys, 'ctx', axis=0, tiled=True)]
    all_to_all x0 -> x1, starting transfers between devices: none -> 7.29 us  [per_device(): lax.all_to_all(jnp.stack([keys] * lax.axis_size('ctx')), 'ctx', 0, 0)]
    cond x72 -> x56, local copies, waits for them, and re-layouts: 33.3 us -> 33.4 us
  transfers between devices with their start and end apart: 3 -> 4, of which waited for: 3 -> 3; matrix products, arithmetic and copies ran while one was open for 1% -> 10% of each run, Pallas kernels for 0% -> 0%
where the time goes in v1:
time: 634 us; the launch traced here: 629 us
  waiting for transfers between devices  385 us (61%)
  local copies, waits for them, and re-layouts  78.5 us (12%)
  matrix products  74.5 us (12%)
  loops' own time  42.1 us (7%)
  other arithmetic  28.2 us (4%)
  between operations  13.8 us (2%)
  starting transfers between devices  7.42 us (1%)
    reduce_scatter x1, waiting for transfers between devices, per_device(): lax.psum_scatter(grad_keys, 'ctx', scatter_dimension=0, tiled=True)  234 us
    all_gather x1, waiting for transfers between devices, per_device(): lax.all_gather(keys, 'ctx', axis=0, tiled=True)  81.6 us
    psum x1, waiting for transfers between devices, per_device(): key_result = lax.psum(own_terms, 'head')  69 us
    dot_general x16, matrix products, block_scores(): jnp.dot(query_rows, key_block.T, preferred_element_type=jnp.float32)  41 us
    cond x56, local copies, waits for them, and re-layouts  33.4 us
    another operation x1, loops' own time, per_device(): carry, unused = lax.scan(first_visit, carry, (blocks, positions))  20.5 us
    another operation x1, loops' own time, second_fold(): lax.scan(second_visit, grad_query, (blocks, positions))  20 us
    squeeze x16, local copies, waits for them, and re-layouts, per_device(): carry, unused = lax.scan(first_visit, carry, (blocks, positions))  15.8 us
  transfers between devices with their start and end apart: 4, of which 3 were waited for; matrix products, arithmetic and copies ran while one was open for 10% of the time, Pallas kernels for 0%

profile of v1, /device:TPU:0, one launch (start us, length us, event | category | flops | bytes accessed | tf_op | source)
XLA Modules:
  0.0 629.5 jit_solution(16193269083397886617)
XLA Ops:
  11.4 7.3 %all-to-all-start = ((bf16[16,224,576]{2,1,0:T(8,128)(2,1)}), bf16[16,224,576]{2,1,0:T(8,128)(2,1)}, u32[]{:S(2)}, u32[]{:S(2)}) async-start(bf16[16,224,576]{2,1,0:T(8,128)(2,1)} %stack.2), calls=%async_computation | async-start | bytes 9175040 | tf_op jit(solution)/shard_map/all_to_all | solution.py:129
  20.0 81.6 %all-gather.2.cloned.1.call-done = bf16[3584,576]{1,0:T(8,128)(2,1)} async-done(((bf16[224,576]{1,0:T(8,128)(2,1)}), bf16[3584,576]{1,0:T(8,128)(2,1)}) %all-gather.2.cloned.1.call-update) | async-done | bytes 4128784 | tf_op jit(solution)/shard_map/all_gather | solution.py:100
  101.6 69.8 %while.31 = (s32[]{:T(128)}, f32[1792]{0:T(1024)S(1)}, f32[1792]{0:T(1024)S(1)}, f32[1792]{0:T(1024)S(1)}, s32[16,224]{1,0:T(8,128)S(1)}, /*index=5*/s32[]{:T(12...) while((s32[]{:T(128)}, f32[1792]{0:T(1024)S(1)}, ...), condition=%wide.region_8.9_spmd.clone, body=%wide.region_1.8_spmd.clone.sunk | while | flops 877082112 | bytes 9882383 | solution.py:123
  103.5 4.8 conditional.6
  114.2 4.8 conditional.6
  123.0 4.8 conditional.6
  129.7 4.8 conditional.6
  142.4 4.8 conditional.6
  151.1 4.8 conditional.6
  157.9 4.8 conditional.6
  164.6 4.8 conditional.6
  173.6 136.9 %while.32 = (s32[]{:T(128)}, f32[1792,576]{0,1:T(8,128)}, f32[16,224,576]{2,1,0:T(8,128)}, s32[16,224]{1,0:T(8,128)S(1)}, s32[]{:T(128)}, /*index=5*/bf16[16,224...) while((s32[]{:T(128)}, f32[1792,576]{0,1:T(8,128)}, ...), condition=%wide.region_13.14_spmd.clone, body=%wide.region_9.13_spmd.clone.sunk | while | flops 2215284992 | bytes 68409680 | solution.py:83
  175.6 11.4 %conditional.7 = (f32[1792,576]{0,1:T(8,128)}, f32[1,224,576]{2,1,0:T(8,128)S(1)}) conditional(s32[]{:T(128)} %convert_element_type.32, f32[1792,576]{0,1:T(8,128)} %get-tuple-element.560, (s32[1,224]{1,0:T(1,128)S(1)}, s32[224]{0:T(256)S(1)}, bf16[16,224,576]{2,1,0:T(8,128)(2,1)}, s32[]{:T(128)}, bf16[1792,576]{1,0:T(8,128)(2,1)}, ...), branch_computations={%region_11.11_spmd, %region_12.12_spmd} | conditional | flops 2215284736 | bytes 67317608 | solution.py:81
  195.5 11.4 %conditional.7 = (f32[1792,576]{0,1:T(8,128)}, f32[1,224,576]{2,1,0:T(8,128)S(1)}) conditional(s32[]{:T(128)} %convert_element_type.32, f32[1792,576]{0,1:T(8,128)} %get-tuple-element.560, (s32[1,224]{1,0:T(1,128)S(1)}, s32[224]{0:T(256)S(1)}, bf16[16,224,576]{2,1,0:T(8,128)(2,1)}, s32[]{:T(128)}, bf16[1792,576]{1,0:T(8,128)(2,1)}, ...), branch_computations={%region_11.11_spmd, %region_12.12_spmd} | conditional | flops 2215284736 | bytes 67317608 | solution.py:81
  212.7 11.4 %conditional.7 = (f32[1792,576]{0,1:T(8,128)}, f32[1,224,576]{2,1,0:T(8,128)S(1)}) conditional(s32[]{:T(128)} %convert_element_type.32, f32[1792,576]{0,1:T(8,128)} %get-tuple-element.560, (s32[1,224]{1,0:T(1,128)S(1)}, s32[224]{0:T(256)S(1)}, bf16[16,224,576]{2,1,0:T(8,128)(2,1)}, s32[]{:T(128)}, bf16[1792,576]{1,0:T(8,128)(2,1)}, ...), branch_computations={%region_11.11_spmd, %region_12.12_spmd} | conditional | flops 2215284736 | bytes 67317608 | solution.py:81
  226.9 11.4 %conditional.7 = (f32[1792,576]{0,1:T(8,128)}, f32[1,224,576]{2,1,0:T(8,128)S(1)}) conditional(s32[]{:T(128)} %convert_element_type.32, f32[1792,576]{0,1:T(8,128)} %get-tuple-element.560, (s32[1,224]{1,0:T(1,128)S(1)}, s32[224]{0:T(256)S(1)}, bf16[16,224,576]{2,1,0:T(8,128)(2,1)}, s32[]{:T(128)}, bf16[1792,576]{1,0:T(8,128)(2,1)}, ...), branch_computations={%region_11.11_spmd, %region_12.12_spmd} | conditional | flops 2215284736 | bytes 67317608 | solution.py:81
  249.7 11.4 %conditional.7 = (f32[1792,576]{0,1:T(8,128)}, f32[1,224,576]{2,1,0:T(8,128)S(1)}) conditional(s32[]{:T(128)} %convert_element_type.32, f32[1792,576]{0,1:T(8,128)} %get-tuple-element.560, (s32[1,224]{1,0:T(1,128)S(1)}, s32[224]{0:T(256)S(1)}, bf16[16,224,576]{2,1,0:T(8,128)(2,1)}, s32[]{:T(128)}, bf16[1792,576]{1,0:T(8,128)(2,1)}, ...), branch_computations={%region_11.11_spmd, %region_12.12_spmd} | conditional | flops 2215284736 | bytes 67317608 | solution.py:81
  266.8 11.4 %conditional.7 = (f32[1792,576]{0,1:T(8,128)}, f32[1,224,576]{2,1,0:T(8,128)S(1)}) conditional(s32[]{:T(128)} %convert_element_type.32, f32[1792,576]{0,1:T(8,128)} %get-tuple-element.560, (s32[1,224]{1,0:T(1,128)S(1)}, s32[224]{0:T(256)S(1)}, bf16[16,224,576]{2,1,0:T(8,128)(2,1)}, s32[]{:T(128)}, bf16[1792,576]{1,0:T(8,128)(2,1)}, ...), branch_computations={%region_11.11_spmd, %region_12.12_spmd} | conditional | flops 2215284736 | bytes 67317608 | solution.py:81
  281.0 11.4 %conditional.7 = (f32[1792,576]{0,1:T(8,128)}, f32[1,224,576]{2,1,0:T(8,128)S(1)}) conditional(s32[]{:T(128)} %convert_element_type.32, f32[1792,576]{0,1:T(8,128)} %get-tuple-element.560, (s32[1,224]{1,0:T(1,128)S(1)}, s32[224]{0:T(256)S(1)}, bf16[16,224,576]{2,1,0:T(8,128)(2,1)}, s32[]{:T(128)}, bf16[1792,576]{1,0:T(8,128)(2,1)}, ...), branch_computations={%region_11.11_spmd, %region_12.12_spmd} | conditional | flops 2215284736 | bytes 67317608 | solution.py:81
  295.3 11.4 %conditional.7 = (f32[1792,576]{0,1:T(8,128)}, f32[1,224,576]{2,1,0:T(8,128)S(1)}) conditional(s32[]{:T(128)} %convert_element_type.32, f32[1792,576]{0,1:T(8,128)} %get-tuple-element.560, (s32[1,224]{1,0:T(1,128)S(1)}, s32[224]{0:T(256)S(1)}, bf16[16,224,576]{2,1,0:T(8,128)(2,1)}, s32[]{:T(128)}, bf16[1792,576]{1,0:T(8,128)(2,1)}, ...), branch_computations={%region_11.11_spmd, %region_12.12_spmd} | conditional | flops 2215284736 | bytes 67317608 | solution.py:81
  310.6 233.6 %reduce-scatter.2.cloned.1.call-done = f32[224,576]{1,0:T(8,128)} async-done(((f32[3584,576]{1,0:T(8,128)}), f32[224,576]{1,0:T(8,128)}) %reduce-scatter.2.cloned.1.call-update) | async-done | bytes 516112 | tf_op jit(solution)/shard_map/reduce_scatter | solution.py:134
  544.2 3.7 convert_element_type.22
  547.9 4.1 copy.7
  552.0 69.0 %all-reduce.3.cloned.1.call-done = f32[224,576]{1,0:T(8,128)} async-done(((f32[224,576]{1,0:T(8,128)}), f32[224,576]{1,0:T(8,128)}) %all-reduce.3.cloned.1.call-update) | async-done | bytes 516112 | tf_op jit(solution)/shard_map/psum | solution.py:135
  (285 shorter events, 174.8 us)
Async XLA Ops:
  7.2 94.4 %all-gather.2.cloned.1.call-start = ((), (), s32[]{:S(2)}) async-start(), calls=%async_computation.2 | async-start | bytes 4874240 | tf_op jit(solution)/shard_map/all_gather | solution.py:100
  11.4 7.5 %copy-start.4 = (s32[32]{0:T(128)S(1)}, s32[32]{0:T(128)}, u32[]{:S(2)}) copy-start(s32[32]{0:T(128)} %param.12) | copy-start | bytes 388
  11.4 90.2 %copy-start.2 = (bf16[224,8,512]{2,1,0:T(8,128)(2,1)S(1)}, bf16[224,8,512]{2,1,0:T(8,128)(2,1)}, u32[]{:S(2)}) copy-start(bf16[224,8,512]{2,1,0:T(8,128)(2,1)} %param.15) | copy-start | bytes 5505028
  11.4 160.1 %all-to-all-start = ((bf16[16,224,576]{2,1,0:T(8,128)(2,1)}), bf16[16,224,576]{2,1,0:T(8,128)(2,1)}, u32[]{:S(2)}, u32[]{:S(2)}) async-start(bf16[16,224,576]{2,1,0:T(8,128)(2,1)} %stack.2), calls=%async_computation | async-start | bytes 9175040 | tf_op jit(solution)/shard_map/all_to_all | solution.py:129
  18.7 525.5 %reduce-scatter.2.cloned.1.call-start = ((), (), s32[]{:S(2)}) async-start(), calls=%async_computation.3 | async-start | bytes 9748480 | tf_op jit(solution)/shard_map/reduce_scatter | solution.py:134
  179.9 1.6 copy-start.3
  181.6 2.2 copy-start
  185.1 1.9 copy-start.1
  199.9 1.6 copy-start.3
  201.6 2.2 copy-start
  205.1 1.9 copy-start.1
  218.7 2.2 copy-start
  222.2 1.9 copy-start.1
  232.9 2.2 copy-start
  236.4 1.9 copy-start.1
  255.8 2.2 copy-start
  259.2 1.9 copy-start.1
  272.9 2.2 copy-start
  276.3 1.9 copy-start.1
  287.1 2.2 copy-start
  290.6 1.9 copy-start.1
  301.3 2.2 copy-start
  304.8 1.9 copy-start.1
  310.5 310.5 %all-reduce.3.cloned.1.call-start = ((), (), s32[]{:S(2)}) async-start(), calls=%async_computation.4 | async-start | bytes 1146880 | tf_op jit(solution)/shard_map/psum | solution.py:135
  (6 other events, 9.9 us)
Sparse Core Ops, SparseCore 0:
  10.4 91.1 all-gather.1
  310.7 233.4 reduce-scatter.1
  546.7 74.2 all-reduce.2
